TPU v7x, 32 devices: a whole 2x2x4 slice. The times are simulated.
32 devices in a mesh: dp: 4 (over x, core), expert: 8 (over z, y).
Axes of the slice: x: 2, y: 2, z: 4, core: 2. Of those that a mesh axis runs over, the one named last changes fastest.
Arguments:
- hidden: bfloat16 [2048, 8, 1536], P(('dp', 'expert')), may hold values from -6 to 6
- routes: int32 [2048, 8], P(('dp', 'expert')), may hold values from 0 to 15, all different within a row; in each aligned block of 64 rows (0 to 63, 64 to 127, ...) at most 48 rows name the same one
- gate_scores: int32 [2048, 8], P(('dp', 'expert')), may hold values from 1 to 64
- down_weight: bfloat16 [16, 1536, 4096], P('expert', None, 'dp'), may hold values from -0.15625 to 0.15625
Outputs:
- output: bfloat16 [2048, 4096], P(('dp', 'expert'))
- gram: float32 [16, 1536, 1536], P('expert', 'dp')
Inputs may be any that keep to these rules, and one draw needn't show every extreme that they name: `routes`: each token names 8 different experts. Among the 64 tokens of one device no expert is named more than 48 times, and on some devices one expert is named exactly 48 times. Every expert is named by some token.
All inputs are finite; a program needn't handle non-finite values.
Results may differ from a plain program's by a relative error of at most 0.005.
Values may be sent and summed in bfloat16 or wider, within the bound.
A program may use at most 128 MiB of HBM per device.

v0:
```python
import jax
import jax.numpy as jnp
from jax import lax
from jax.sharding import PartitionSpec as P


def local(hidden, routes, gate_scores, down_weight):
    tokens = hidden.shape[0]
    top_count = hidden.shape[1]
    hidden_width = hidden.shape[2]
    n_owner = lax.axis_size("expert")
    n_group = lax.axis_size("dp")
    per_owner = down_weight.shape[0]
    experts = n_owner * per_owner
    pair_total = tokens * top_count
    capacity = 3 * tokens * top_count // (2 * experts)
    flat_routes = routes.reshape(pair_total)
    onehot = (flat_routes[:, None] == jnp.arange(experts, dtype=jnp.int32)[None, :]).astype(
        jnp.int32
    )
    before = jnp.cumsum(onehot, axis=0) - onehot
    position = jnp.sum(before * onehot, axis=1)
    slot_index = flat_routes * capacity + position
    local_counts = jnp.sum(onehot, axis=0).astype(jnp.float32)
    totals = lax.psum(local_counts, ("dp", "expert"))
    pair_rows = hidden.reshape(pair_total, hidden_width)
    outgoing = (
        jnp.zeros((experts * capacity, hidden_width), jnp.bfloat16).at[slot_index].set(pair_rows)
    )
    outgoing = outgoing.reshape(n_owner, per_owner, capacity, hidden_width)
    arrived = lax.all_to_all(outgoing, "expert", split_axis=0, concat_axis=0, tiled=True)
    everyone = lax.all_gather(arrived, "dp", axis=0, tiled=True)
    own_counts = lax.dynamic_slice_in_dim(
        totals, lax.axis_index("expert") * per_owner, per_owner, 0
    )
    block_width = hidden_width // n_group
    my_columns = lax.dynamic_slice_in_dim(
        everyone, lax.axis_index("dp") * block_width, block_width, 3
    )
    gram_rows = jnp.einsum(
        "sxcf,sxcg->xfg", my_columns, everyone, preferred_element_type=jnp.float32
    )
    results = jnp.einsum(
        "sxcf,xfd->sxcd", everyone, down_weight, preferred_element_type=jnp.float32
    ).astype(jnp.bfloat16)
    returned = lax.all_to_all(
        lax.all_to_all(results, "dp", split_axis=0, concat_axis=3, tiled=True),
        "expert",
        split_axis=0,
        concat_axis=0,
        tiled=True,
    )
    gram = gram_rows / own_counts[:, None, None]
    model_width = returned.shape[3]
    pair_results = returned.reshape(experts * capacity, model_width)[slot_index]
    scores = gate_scores.astype(jnp.float32)
    weight = scores / jnp.sum(scores, axis=1, keepdims=True)
    combined = jnp.sum(
        pair_results.reshape(tokens, top_count, model_width).astype(jnp.float32)
        * weight[:, :, None],
        axis=1,
    )
    return (combined.astype(jnp.bfloat16), gram)


def solution(mesh):
    placed = (
        P(("dp", "expert"), None, None),
        P(("dp", "expert"), None),
        P(("dp", "expert"), None),
        P("expert", None, "dp"),
    )
    return jax.shard_map(
        local,
        mesh=mesh,
        in_specs=placed,
        out_specs=(P(("dp", "expert"), None), P("expert", "dp", None)),
        check_vma=False,
    )
```

profile of v0, /device:TPU:1, one launch (start us, length us, event | category | flops | bytes accessed | tf_op | source)
XLA Modules:
  0.0 451.6 jit_solution(3097682405529023763)
XLA Ops:
  7.2 0.9 copy.15
  8.1 0.1 eq.29
  8.2 0.1 eq.25
  8.3 0.7 broadcast_multiply_fusion
  9.0 1.1 reduce-window.6
  10.1 0.2 slice_reduce_fusion
  10.4 0.1 copy.14
  10.5 0.1 mul.35
  10.6 0.1 convert_reduce_fusion
  10.7 4.7 %scatter_custom_fusion = bf16[768,1536]{1,0:T(8,128)(2,1)} fusion(s32[512]{0:T(512)S(1)} %bitcast.42, bf16[64,8,1536]{2,1,0:T(8,128)(2,1)S(1)} %copy-done, bf16[]{:T(256)} %constant.11.clone.1), kind=kCustom, calls=%fused_computation.10 | custom fusion | bytes 3932162 | tf_op jit(solution)/shard_map/scatter | solution.py:28
  15.4 59.3 %all_to_all.28 = bf16[8,2,48,1536]{3,2,1,0:T(8,128)(2,1)S(1)} all-to-all(bf16[8,2,48,1536]{3,2,1,0:T(8,128)(2,1)} %bitcast.41), channel_id=1, replica_groups=mesh['dp'=4,'expert'=8] {'expert'}, dimensions={0} | all-to-all | bytes 4718592 | tf_op jit(solution)/shard_map/all_to_all | solution.py:31
  74.7 1.6 copy.18
  76.3 65.0 %all-gather.2.cloned.1.call-done = bf16[32,2,48,1536]{3,2,0,1:T(8,128)(2,1)} async-done(((bf16[8,2,48,1536]{3,2,0,1:T(8,128)(2,1)}), bf16[32,2,48,1536]{3,2,0,1:T(8,128)(2,1)}) %all-gather.2.cloned.1.call-update) | async-done | bytes 9437200 | tf_op jit(solution)/shard_map/all_gather | solution.py:32
  141.3 14.3 %convert_bitcast_fusion = bf16[32,2,48,1024]{3,2,0,1:T(8,128)(2,1)S(1)} fusion(bf16[32,2,48,1536]{3,2,0,1:T(8,128)(2,1)} %all-gather.2.cloned.1.call-done, bf16[2,1536,1024]{2,1,0:T(8,128)(2,1)} %param.7), kind=kOutput, calls=%fused_computation.7 | convolution fusion | flops 9666822144 | bytes 22020096 | tf_op jit(solution)/shard_map/sxcf,xfd->sxcd/dot_general | solution.py:43
  155.6 1.3 copy.19
  156.9 73.4 %all_to_all.29 = bf16[32,2,48,1024]{3,2,1,0:T(8,128)(2,1)} all-to-all(bf16[32,2,48,1024]{3,2,1,0:T(8,128)(2,1)S(1)} %copy.19), channel_id=1, replica_groups=mesh['dp'=4,'expert'=8] {'dp'}, dimensions={0} | all-to-all | bytes 12582912 | tf_op jit(solution)/shard_map/all_to_all | solution.py:47
  230.3 10.8 %copy.27 = bf16[4,8,2,48,1024]{4,0,3,2,1:T(4,128)(2,1)} copy(bf16[4,8,2,48,1024]{4,3,2,1,0:T(8,128)(2,1)} %bitcast.39) | data formatting | bytes 12582912 | tf_op jit(solution)/shard_map/all_to_all | solution.py:47
  241.1 11.1 %all_to_all.23 = bf16[8,2,48,4096]{3,2,1,0:T(8,128)(2,1)} reshape(bf16[8,2,48,4,1024]{4,3,2,1,0:T(4,128)(2,1)} %bitcast.40) | data formatting | bytes 12582912 | tf_op jit(solution)/shard_map/all_to_all | solution.py:47
  252.2 5.4 %all-to-all-start.2 = ((bf16[8,2,48,4096]{3,2,1,0:T(8,128)(2,1)}), bf16[8,2,48,4096]{3,2,1,0:T(8,128)(2,1)}, u32[]{:S(2)}, u32[]{:S(2)}) async-start(bf16[8,2,48,4096]{3,2,1,0:T(8,128)(2,1)} %all_to_all.23), calls=%async_computation.2 | async-start | bytes 12582912 | tf_op jit(solution)/shard_map/all_to_all | solution.py:46
  257.6 157.7 %psum.7 = f32[16]{0:T(128)S(1)} all-reduce(f32[16]{0:T(128)S(1)} %convert_element_type.36), channel_id=1, replica_groups=mesh['dp'=4,'expert'=8] {'dp','expert'}, use_global_device_ids=true, to_apply=%region_7.8 | all-reduce | flops 16 | bytes 128 | tf_op jit(solution)/shard_map/psum | solution.py:25
  415.4 0.1 copy.21
  415.5 10.5 %bitcast_divide_fusion = f32[2,384,1536]{2,1,0:T(8,128)} fusion(bf16[32,2,48,1536]{3,2,0,1:T(8,128)(2,1)} %all-gather.2.cloned.1.call-done, f32[2]{0:T(128)S(1)} %dynamic_slice.7, s32[]{:T(128)S(6)} %select_n.18), kind=kOutput, calls=%fused_computation.8 | convolution fusion | flops 3625058304 | bytes 16515084 | tf_op jit(solution)/shard_map/sxcf,sxcg->xfg/dot_general | solution.py:40
  426.0 12.3 %gather_fusion = bf16[512,4096]{1,0:T(8,128)(2,1)} fusion(bf16[768,4096]{1,0:T(8,128)(2,1)} %bitcast.10, s32[1024]{0:T(1024)S(1)} %pad_clamp_fusion), kind=kCustom, calls=%fused_computation | custom fusion | bytes 8390656 | tf_op jit(solution)/shard_map/gather | solution.py:55
  438.3 6.5 %fusion = bf16[64,4096]{1,0:T(8,128)(2,1)} fusion(bf16[512,4096]{1,0:T(8,128)(2,1)} %gather_fusion, f32[64,8]{1,0:T(8,128)S(1)} %copy.21), kind=kLoop, calls=%fused_computation.3 | loop fusion | flops 6029312 | bytes 4720640 | tf_op jit(solution)/shard_map/reduce_sum | solution.py:58
  (18 shorter events, 0.2 us)
Async XLA Ops:
  7.2 3.6 copy-start
  7.2 134.1 %all-gather.2.cloned.1.call-start = ((), (), s32[]{:S(2)}) async-start(), calls=%async_computation.3 | async-start | bytes 11796480 | tf_op jit(solution)/shard_map/all_gather | solution.py:32
  252.2 163.1 %copy-start.2 = (s32[64,8]{0,1:T(8,128)S(1)}, s32[64,8]{0,1:T(8,128)}, u32[]{:S(2)}) copy-start(s32[64,8]{0,1:T(8,128)} %param.6) | copy-start | bytes 6148
  252.2 173.8 %all-to-all-start.2 = ((bf16[8,2,48,4096]{3,2,1,0:T(8,128)(2,1)}), bf16[8,2,48,4096]{3,2,1,0:T(8,128)(2,1)}, u32[]{:S(2)}, u32[]{:S(2)}) async-start(bf16[8,2,48,4096]{3,2,1,0:T(8,128)(2,1)} %all_to_all.23), calls=%async_computation.2 | async-start | bytes 12582912 | tf_op jit(solution)/shard_map/all_to_all | solution.py:46
  426.0 18.7 %copy-start.1 = (bf16[64,8,1536]{2,1,0:T(8,128)(2,1)S(1)}, bf16[64,8,1536]{2,1,0:T(8,128)(2,1)}, u32[]{:S(2)}) copy-start(bf16[64,8,1536]{2,1,0:T(8,128)(2,1)} %param.4) | copy-start | bytes 4718596
Sparse Core Ops, SparseCore 0:
  76.4 64.8 all-gather.1
where the time goes:
time: 454 us; the launch traced here: 452 us
  blocking collectives  290 us (64%)
  waiting for transfers between devices  65 us (14%)
  local copies, waits for them, and re-layouts  43.3 us (10%)
  matrix products  24.8 us (5%)
  between operations  14.1 us (3%)
  other arithmetic  8.53 us (2%)
  starting transfers between devices  5.41 us (1%)
    psum x1, blocking collectives, local(): totals = lax.psum(local_counts, ('dp', 'expert'))  158 us
    all_to_all x1, blocking collectives, local(): lax.all_to_all(results, 'dp', split_axis=0, concat_axis=3, tiled=True)  73.4 us
    all_gather x1, waiting for transfers between devices, local(): everyone = lax.all_gather(arrived, 'dp', axis=0, tiled=True)  65 us
    all_to_all x1, blocking collectives, local(): lax.all_to_all(outgoing, 'expert', split_axis=0, concat_axis=0, tiled=True)  59.3 us
    all_to_all x2, local copies, waits for them, and re-layouts, local(): lax.all_to_all(results, 'dp', split_axis=0, concat_axis=3, tiled=True)  21.9 us
    dot_general x1, matrix products, local(): jnp.einsum('sxcf,xfd->sxcd', everyone, down_weight, preferred_element_typ...  14.3 us
    gather x1, local copies, waits for them, and re-layouts, local(): pair_results = returned.reshape(experts * capacity, model_width)[slot_index]  12.3 us
    dot_general x1, matrix products, local(): jnp.einsum('sxcf,sxcg->xfg', my_columns, everyone, preferred_element_type...  10.5 us
  transfers between devices with their start and end apart: 2, of which 1 were waited for; matrix products, arithmetic and copies ran while one was open for 2% of the time, Pallas kernels for 0%

commit v1 on v0

--- a/solution.py
+++ b/solution.py
@@ -1,10 +1,322 @@
+import functools
+
 import jax
 import jax.numpy as jnp
 from jax import lax
+from jax.experimental import pallas as pl
+from jax.experimental.pallas import tpu as pltpu
 from jax.sharding import PartitionSpec as P
 
-
-def local(hidden, routes, gate_scores, down_weight):
+MESH = pl.DeviceIdType.MESH
+META = 128
+TILE = 256
+VMEM_BUDGET = 58 * 2**20
+VMEM_LIMIT = 63 * 2**20
+
+
+def fused_kernel(
+    nd, ne, tokens, cap, width,
+    og, w_hbm, o_ref, g_ref, c_ref,
+    buf, w, sendy, recvy, keep, sendz, recvz, fin, osc, chi, clo,
+    wsem, lsem, asend, xsend, csend, recv, ysend, yrecv, zsend, zrecv, osend, orecv,
+):
+    po = w.shape[0]
+    nz = ne // 2
+    nx = nd // 2
+    rows = nd * cap
+    group = nd * tokens
+    cols = w.shape[2]
+    d = lax.axis_index("dp")
+    e = lax.axis_index("expert")
+    x, c = lax.div(d, 2), lax.rem(d, 2)
+    z, y = lax.div(e, 2), lax.rem(e, 2)
+    other = d + 1 - 2 * c
+    pair = e + 1 - 2 * y
+
+    load_w = pltpu.make_async_copy(w_hbm, w, wsem)
+    load_w.start()
+
+    def slot_of(dd, ee):
+        return buf.at[:, pl.ds(pl.multiple_of((ee * nd + dd) * cap, cap), cap), :]
+
+    own = pltpu.make_async_copy(
+        og.at[pl.ds(e * po, po)], slot_of(d, e), lsem
+    )
+    own.start()
+
+    barrier = pltpu.get_barrier_semaphore()
+    for k in range(1, ne):
+        pl.semaphore_signal(
+            barrier, inc=1, device_id=(d, lax.rem(e + k, ne)), device_id_type=MESH
+        )
+    for k in range(1, nd):
+        pl.semaphore_signal(
+            barrier, inc=1, device_id=(lax.rem(d + k, nd), e), device_id_type=MESH
+        )
+    pl.semaphore_wait(barrier, ne - 1 + nd - 1)
+
+    def remote(src, dst, ss, rs, dd, ee):
+        return pltpu.make_async_remote_copy(
+            src_ref=src, dst_ref=dst, send_sem=ss, recv_sem=rs,
+            device_id=(dd, ee), device_id_type=MESH,
+        )
+
+    def first(i):
+        kz, ky = (i // 2 + 1) % nz, i % 2
+        target = lax.rem(z + kz, nz) * 2 + lax.rem(y + ky, 2)
+        return remote(
+            og.at[pl.ds(target * po, po)], slot_of(d, e), asend.at[i],
+            recv.at[e * nd + d], d, target,
+        )
+
+    for i in range(ne):
+        if i != ne - 2:
+            first(i).start()
+    own.wait()
+    c_ref[...] = jnp.zeros_like(c_ref)
+
+    def source_of(i):
+        kz = lax.rem(lax.div(i, 2) + 1, nz)
+        zi = lax.rem(z - kz + nz, nz)
+        return zi, zi * 2 + lax.rem(y + lax.rem(i, 2), 2)
+
+    def arrived(dd, ee):
+        here = slot_of(dd, ee)
+        remote(here, here, asend.at[0], recv.at[ee * nd + dd], d, e).wait_recv()
+
+    def to_x(i, j, ee):
+        here = slot_of(d, ee)
+        return remote(
+            here, here, xsend.at[i, j], recv.at[ee * nd + d],
+            lax.rem(x + j + 1, nx) * 2 + c, e,
+        )
+
+    def to_core(i, j, ee):
+        dd = lax.rem(x + j, nx) * 2 + c
+        here = slot_of(dd, ee)
+        return remote(here, here, csend.at[i, j], recv.at[ee * nd + dd], other, e)
+
+    def to_pair(zi):
+        return remote(sendy.at[zi], recvy.at[zi], ysend.at[zi], yrecv.at[zi], d, pair)
+
+    def to_line(zi):
+        return remote(
+            sendz.at[zi], recvz.at[z], zsend.at[zi], zrecv.at[z], d, zi * 2 + y
+        )
+
+    def from_pair(zi):
+        remote(sendy.at[zi], recvy.at[zi], ysend.at[zi], yrecv.at[zi], d, e).wait_recv()
+
+    def work(i):
+        zi, ee = source_of(i)
+        mine = lax.rem(i, 2) == 0
+        span = pl.ds(pl.multiple_of(ee * rows, rows), rows)
+        row = lax.broadcasted_iota(jnp.int32, (rows, 1), 0)
+        base = jnp.zeros((rows, 1), jnp.int32)
+        for k in range(1, nd):
+            base = base + jnp.where(row >= k * cap, tokens, 0)
+        col = lax.broadcasted_iota(jnp.int32, (rows, group), 1)
+        for q in range(po):
+            meta = buf[q, span, width:width + META].astype(jnp.float32)
+            hit = col == meta[:, 0:1].astype(jnp.int32) + base
+            chi[q] = jnp.where(hit, meta[:, 1:2], 0.0).astype(jnp.bfloat16)
+            clo[q] = jnp.where(hit, meta[:, 2:3], 0.0).astype(jnp.bfloat16)
+            c_ref[q] = c_ref[q] + jnp.sum(meta[:, 3:4], axis=0, keepdims=True)
+
+        @pl.loop(0, cols // TILE)
+        def _(t):
+            cs = pl.ds(pl.multiple_of(t * TILE, TILE), TILE)
+            acc = jnp.zeros((group, TILE), jnp.float32)
+            for q in range(po):
+                h = jnp.dot(
+                    buf[q, span, 0:width], w[q, :, cs], preferred_element_type=jnp.float32
+                ).astype(jnp.bfloat16)
+                for part in (chi, clo):
+                    acc = acc + lax.dot_general(
+                        part[q], h, (((0,), (0,)), ((), ())),
+                        preferred_element_type=jnp.float32,
+                    )
+
+            @pl.when(mine)
+            def _():
+                keep[zi, :, cs] = acc
+
+            @pl.when(jnp.logical_not(mine))
+            def _():
+                sendy[zi, :, cs] = acc.astype(jnp.bfloat16)
+
+        @pl.when(jnp.logical_not(mine))
+        def _():
+            to_pair(zi).start()
+
+            @pl.when(i >= 3)
+            def _():
+                zp, _ = source_of(i - 2)
+                from_pair(zp)
+                sendz[zp] = (keep[zp] + recvy[zp].astype(jnp.float32)).astype(jnp.bfloat16)
+                to_line(zp).start()
+
+    load_w.wait()
+
+    def step(i, carry):
+        @pl.when(i < ne)
+        def _():
+            _, ee = source_of(i)
+
+            @pl.when(i != ne - 2)
+            def _():
+                arrived(d, ee)
+
+            for j in range(nx - 1):
+                to_x(i, j, ee).start()
+            to_core(i, 0, ee).start()
+
+        @pl.when(jnp.logical_and(i >= 1, i < ne + 1))
+        def _():
+            _, ee = source_of(i - 1)
+            for j in range(1, nx):
+                arrived(lax.rem(x + j, nx) * 2 + c, ee)
+                to_core(i - 1, j, ee).start()
+
+        @pl.when(i >= 2)
+        def _():
+            _, ee = source_of(i - 2)
+            for j in range(nx):
+                arrived(lax.rem(x + j, nx) * 2 + 1 - c, ee)
+            work(i - 2)
+
+        return carry
+
+    lax.fori_loop(0, ne + 2, step, 0)
+
+    block = g_ref.shape[1]
+    for q in range(po):
+        @pl.loop(0, width // TILE)
+        def _(t):
+            cs = pl.ds(pl.multiple_of(t * TILE, TILE), TILE)
+            g_ref[q, :, cs] = lax.dot_general(
+                buf[q, :, pl.ds(pl.multiple_of(d * block, block), block)],
+                buf[q, :, cs],
+                (((0,), (0,)), ((), ())),
+                preferred_element_type=jnp.float32,
+            )
+
+    from_pair(z)
+    for k in range(1, nz):
+        zk = lax.rem(z + k, nz)
+        remote(sendz.at[zk], recvz.at[zk], zsend.at[zk], zrecv.at[zk], d, e).wait_recv()
+
+    @pl.loop(0, nd)
+    def _(k):
+        rs = pl.ds(pl.multiple_of(k * tokens, tokens), tokens)
+        total = keep[z, rs, :] + recvy[z, rs, :].astype(jnp.float32)
+        for j in range(1, nz):
+            total = total + recvz[lax.rem(z + j, nz), rs, :].astype(jnp.float32)
+        fin[k] = total.astype(jnp.bfloat16)
+
+    def to_token(k):
+        dd = lax.rem(d + k, nd)
+        return remote(fin.at[dd], osc.at[d], osend.at[k], orecv.at[d], dd, e)
+
+    for k in range(1, nd):
+        to_token(k).start()
+    o_ref[:, pl.ds(pl.multiple_of(d * cols, cols), cols)] = fin[d]
+    for k in range(1, nd):
+        dd = lax.rem(d + k, nd)
+        remote(fin.at[dd], osc.at[dd], osend.at[k], orecv.at[dd], d, e).wait_recv()
+        o_ref[:, pl.ds(pl.multiple_of(dd * cols, cols), cols)] = osc[dd]
+
+    for i in range(ne):
+        if i != ne - 2:
+            first(i).wait_send()
+
+    def drain(i, carry):
+        _, ee = source_of(i)
+        for j in range(nx - 1):
+            to_x(i, j, ee).wait_send()
+        for j in range(nx):
+            to_core(i, j, ee).wait_send()
+        return carry
+
+    lax.fori_loop(0, ne, drain, 0)
+    for k in range(nz):
+        to_pair(k).wait_send()
+    for k in range(1, nz):
+        to_line(lax.rem(z + k, nz)).wait_send()
+    for k in range(1, nd):
+        to_token(k).wait_send()
+
+
+def positions(routes, experts):
+    flat_routes = routes.reshape(-1)
+    onehot = (flat_routes[:, None] == jnp.arange(experts, dtype=jnp.int32)[None, :]).astype(
+        jnp.int32
+    )
+    before = jnp.cumsum(onehot, axis=0) - onehot
+    return flat_routes, onehot, jnp.sum(before * onehot, axis=1)
+
+
+def fused(hidden, routes, gate_scores, down_weight):
+    tokens, top_count, width = hidden.shape
+    ne, nd = lax.axis_size("expert"), lax.axis_size("dp")
+    po, _, cols = down_weight.shape
+    experts = ne * po
+    pairs = tokens * top_count
+    cap = 3 * pairs // (2 * experts)
+    flat_routes, _, position = positions(routes, experts)
+    slot_index = flat_routes * cap + position
+    scores = gate_scores.astype(jnp.float32)
+    weight = (scores / jnp.sum(scores, axis=1, keepdims=True)).reshape(pairs)
+    hi = weight.astype(jnp.bfloat16)
+    lo = (weight - hi.astype(jnp.float32)).astype(jnp.bfloat16)
+    token = (jnp.arange(pairs, dtype=jnp.int32) // top_count).astype(jnp.bfloat16)
+    meta = jnp.stack([token, hi, lo, jnp.ones_like(hi)], axis=1)
+    meta = jnp.pad(meta, ((0, 0), (0, META - 4)))
+    pick = (
+        jnp.arange(experts * cap, dtype=jnp.int32)[:, None] == slot_index[None, :]
+    ).astype(jnp.bfloat16)
+    packed = jnp.concatenate([hidden.reshape(pairs, width), meta], axis=1)
+    outgoing = jnp.dot(pick, packed, preferred_element_type=jnp.float32).astype(jnp.bfloat16)
+    outgoing = outgoing.reshape(experts, cap, width + META)
+
+    nz, nx, group = ne // 2, nd // 2, nd * tokens
+    bf, f32 = jnp.bfloat16, jnp.float32
+    dma = pltpu.SemaphoreType.DMA
+    any_space = pl.BlockSpec(memory_space=pl.ANY)
+    vmem = pl.BlockSpec(memory_space=pltpu.VMEM)
+    out, gram, count = pl.pallas_call(
+        functools.partial(fused_kernel, nd, ne, tokens, cap, width),
+        out_shape=(
+            jax.ShapeDtypeStruct((tokens, nd * cols), bf),
+            jax.ShapeDtypeStruct((po, width // nd, width), f32),
+            jax.ShapeDtypeStruct((po, 8, 128), f32),
+        ),
+        in_specs=[vmem, any_space],
+        out_specs=(vmem, vmem, vmem),
+        scratch_shapes=[
+            pltpu.VMEM((po, ne * nd * cap, width + META), bf),
+            pltpu.VMEM((po, width, cols), bf),
+            pltpu.VMEM((nz, group, cols), bf),
+            pltpu.VMEM((nz, group, cols), bf),
+            pltpu.VMEM((nz, group, cols), f32),
+            pltpu.VMEM((nz, group, cols), bf),
+            pltpu.VMEM((nz, group, cols), bf),
+            pltpu.VMEM((nd, tokens, cols), bf),
+            pltpu.VMEM((nd, tokens, cols), bf),
+            pltpu.VMEM((po, nd * cap, group), bf),
+            pltpu.VMEM((po, nd * cap, group), bf),
+            dma, dma,
+            dma((ne,)), dma((ne, max(nx - 1, 1))), dma((ne, nx)), dma((ne * nd,)),
+            dma((nz,)), dma((nz,)), dma((nz,)), dma((nz,)), dma((nd,)), dma((nd,)),
+        ],
+        compiler_params=pltpu.CompilerParams(
+            collective_id=0, has_side_effects=True, vmem_limit_bytes=VMEM_LIMIT
+        ),
+    )(outgoing, down_weight)
+    return out, gram / count[:, :1, :1]
+
+
+def plain(hidden, routes, gate_scores, down_weight):
     tokens = hidden.shape[0]
     top_count = hidden.shape[1]
     hidden_width = hidden.shape[2]
@@ -63,6 +375,32 @@
     return (combined.astype(jnp.bfloat16), gram)
 
 
+def fits(hidden, down_weight, nd, ne):
+    tokens, top_count, width = hidden.shape
+    po, _, cols = down_weight.shape
+    cap = 3 * tokens * top_count // (2 * ne * po)
+    group = nd * tokens
+    if cap % 16 or tokens % 16 or nd % 2 or ne % 2 or ne < 4 or tokens > 256:
+        return False
+    if width % TILE or cols % TILE or (width // nd) % 128:
+        return False
+    need = (
+        2 * po * ne * cap * (nd + 1) * (width + META)
+        + 2 * po * width * cols
+        + (ne // 2) * group * cols * 12
+        + 4 * po * (width // nd) * width
+        + 6 * group * cols
+        + 4 * po * nd * cap * group
+    )
+    return need <= VMEM_BUDGET
+
+
+def local(hidden, routes, gate_scores, down_weight):
+    if fits(hidden, down_weight, lax.axis_size("dp"), lax.axis_size("expert")):
+        return fused(hidden, routes, gate_scores, down_weight)
+    return plain(hidden, routes, gate_scores, down_weight)
+
+
 def solution(mesh):
     placed = (
         P(("dp", "expert"), None, None),

time: 454 us -> 152 us (0.33)
  blocking collectives: 290 us -> 0 us
  Pallas kernels: 0 us -> 136 us
  waiting for transfers between devices: 65 us -> 0 us
  local copies, waits for them, and re-layouts: 43.3 us -> 3.19 us
  matrix products: 24.8 us -> 4.5 us
  between operations: 14.1 us -> 0.67 us
  starting transfers between devices: 5.41 us -> 0 us
    psum x1 -> x0, blocking collectives: 158 us -> none  [local(): totals = lax.psum(local_counts, ('dp', 'expert'))]
    pallas_call x0 -> x1, Pallas kernels: none -> 136 us  [fused(): pl.pallas_call(functools.partial(fused_kernel, nd, ne, tokens, cap, width...]
    all_to_all x2 -> x0, blocking collectives: 133 us -> none  [the longest x1 73.4 us: local(): lax.all_to_all(results, 'dp', split_axis=0, concat_axis=3, tiled=True)]
    all_gather x1 -> x0, waiting for transfers between devices: 65 us -> none  [local(): everyone = lax.all_gather(arrived, 'dp', axis=0, tiled=True)]
    all_to_all x3 -> x0, local copies, waits for them, and re-layouts: 23.4 us -> none  [the longest x2 21.9 us: local(): lax.all_to_all(results, 'dp', split_axis=0, concat_axis=3, tiled=True)]
    dot_general x2 -> x1, matrix products: 24.8 us -> 4.5 us  [fused(): jnp.dot(pick, packed, preferred_element_type=jnp.float32)]
    gather x1 -> x0, local copies, waits for them, and re-layouts: 12.3 us -> none  [local(): pair_results = returned.reshape(experts * capacity, model_width)[slot_index]]
    div x1 -> x2, other arithmetic: 0.01 us -> 5.88 us  [the longest x1 5.19 us: fused(): return (out, gram / count[:, :1, :1])]
  transfers between devices with their start and end apart: 2 -> 0, of which waited for: 1 -> 0; matrix products, arithmetic and copies ran while one was open for 2% -> 0% of each run, Pallas kernels for 0% -> 0%
where the time goes in v1:
time: 152 us
  Pallas kernels  136 us (89%)
  other arithmetic  7.98 us (5%)
  matrix products  4.5 us (3%)
  local copies, waits for them, and re-layouts  3.19 us (2%)
    pallas_call x1, Pallas kernels, fused(): pl.pallas_call(functools.partial(fused_kernel, nd, ne, tokens, cap, width...  136 us
    div x1, other arithmetic, fused(): return (out, gram / count[:, :1, :1])  5.19 us
    dot_general x1, matrix products, fused(): jnp.dot(pick, packed, preferred_element_type=jnp.float32)  4.5 us

profile of v1, /device:TPU:1, one launch (start us, length us, event | category | flops | bytes accessed | tf_op | source)
XLA Modules:
  0.0 151.9 jit_solution(3092974939856274614)
XLA Ops:
  0.6 0.7 convert_reduce_fusion
  1.3 0.1 pad.10.clone
  1.4 0.7 convert_divide_fusion
  2.1 0.1 copy.9
  2.2 0.1 reshape.111
  2.3 0.1 maximum_maximum_fusion
  2.4 0.8 copy.6
  3.2 0.1 reshape.108
  3.2 0.1 eq.40
  3.4 1.2 reduce-window.6
  4.5 0.2 slice_reduce_fusion
  4.8 0.1 fusion.10
  4.9 0.2 copy.11
  5.1 4.5 %convolution_convert_fusion = bf16[768,1664]{1,0:T(8,128)(2,1)} fusion(bf16[512,4]{1,0:T(8,128)(2,1)S(1)} %copy.11, bf16[512,1536]{1,0:T(8,128)(2,1)} %bitcast.23, s32[512]{0:T(512)S(1)} %multiply_add_fusion), kind=kOutput, calls=%fused_computation.2 | convolution fusion | flops 1315405824 | bytes 4134912 | tf_op jit(solution)/shard_map/dot_general | solution.py:279
  9.6 135.6 %shard_map.59 = (bf16[64,4096]{1,0:T(8,128)(2,1)}, f32[2,384,1536]{2,1,0:T(8,128)}, f32[2,8,128]{2,1,0:T(8,128)}) custom-call(bf16[16,48,1664]{2,1,0:T(8,128)(2,1)} %bitcast.22, bf16[2,1536,1024]{2,1,0:T(8,128)(2,1)} %w_hbm.1), custom_call_target="tpu_custom_call" | custom-call | tf_op jit(solution)/shard_map/pallas_call | solution.py:287
  145.1 0.8 slice_reduce_fusion.1
  145.9 0.0 copy-start
  145.9 5.2 %broadcast_divide_fusion = f32[2,384,1536]{2,1,0:T(8,128)} fusion(f32[2,384,1536]{2,1,0:T(8,128)} %get-tuple-element.6, f32[2]{0:T(128)S(1)} %slice_reduce_fusion.1), kind=kLoop, calls=%fused_computation.3 | loop fusion | flops 1179648 | bytes 9437192 | tf_op jit(solution)/shard_map/div | solution.py:316
  151.1 0.0 copy-done
  151.1 0.8 copy.15
  (6 shorter events, 0.1 us)
Async XLA Ops:
  145.9 5.2 %copy-start = (bf16[64,4096]{1,0:T(8,128)(2,1)S(1)}, bf16[64,4096]{1,0:T(8,128)(2,1)}, u32[]{:S(2)}) copy-start(bf16[64,4096]{1,0:T(8,128)(2,1)} %get-tuple-element.12) | copy-start | bytes 1572868

commit v2 on v1

--- a/solution.py
+++ b/solution.py
@@ -61,24 +61,27 @@
             device_id=(dd, ee), device_id_type=MESH,
         )
 
+    near = z + 1 - 2 * lax.rem(z, 2)
+    far = lax.rem(z + 2, nz)
+
+    def source_of(i):
+        j = lax.div(i, 2)
+        flip = lax.rem(j, 2) * (1 - 2 * lax.rem(z, 2))
+        zi = lax.rem(z + flip + 2 * lax.rem(lax.div(j + 1, 2), 2), nz)
+        return zi, zi * 2 + lax.rem(y + lax.rem(i, 2), 2)
+
     def first(i):
-        kz, ky = (i // 2 + 1) % nz, i % 2
-        target = lax.rem(z + kz, nz) * 2 + lax.rem(y + ky, 2)
+        _, target = source_of(jnp.int32(i))
         return remote(
             og.at[pl.ds(target * po, po)], slot_of(d, e), asend.at[i],
             recv.at[e * nd + d], d, target,
         )
 
-    for i in range(ne):
-        if i != ne - 2:
-            first(i).start()
+    for i in range(1, ne):
+        first(i).start()
     own.wait()
     c_ref[...] = jnp.zeros_like(c_ref)
-
-    def source_of(i):
-        kz = lax.rem(lax.div(i, 2) + 1, nz)
-        zi = lax.rem(z - kz + nz, nz)
-        return zi, zi * 2 + lax.rem(y + lax.rem(i, 2), 2)
+    g_ref[...] = jnp.zeros_like(g_ref)
 
     def arrived(dd, ee):
         here = slot_of(dd, ee)
@@ -96,16 +99,42 @@
         here = slot_of(dd, ee)
         return remote(here, here, csend.at[i, j], recv.at[ee * nd + dd], other, e)
 
-    def to_pair(zi):
-        return remote(sendy.at[zi], recvy.at[zi], ysend.at[zi], yrecv.at[zi], d, pair)
-
-    def to_line(zi):
+    def chunk(k):
+        return pl.ds(pl.multiple_of(k * tokens, tokens), tokens)
+
+    def to_pair(zi, k):
         return remote(
-            sendz.at[zi], recvz.at[z], zsend.at[zi], zrecv.at[z], d, zi * 2 + y
-        )
-
-    def from_pair(zi):
-        remote(sendy.at[zi], recvy.at[zi], ysend.at[zi], yrecv.at[zi], d, e).wait_recv()
+            sendy.at[zi, chunk(k)], recvy.at[zi, chunk(k)],
+            ysend.at[zi, k], yrecv.at[zi, k], d, pair,
+        )
+
+    def from_pair(zi, k):
+        remote(
+            sendy.at[zi, chunk(k)], recvy.at[zi, chunk(k)],
+            ysend.at[zi, k], yrecv.at[zi, k], d, e,
+        ).wait_recv()
+
+    def to_line(m, k, zt):
+        return remote(
+            sendz.at[m, chunk(k)], recvz.at[m, chunk(k)],
+            zsend.at[m, k], zrecv.at[m, k], d, zt * 2 + y,
+        )
+
+    def from_line(m, k):
+        remote(
+            sendz.at[m, chunk(k)], recvz.at[m, chunk(k)],
+            zsend.at[m, k], zrecv.at[m, k], d, e,
+        ).wait_recv()
+
+    def both(zi, k):
+        return keep[zi, chunk(k), :] + recvy[zi, chunk(k), :].astype(jnp.float32)
+
+    def chunks(body):
+        def at(k, carry):
+            body(lax.rem(d + 1 + k, nd))
+            return carry
+
+        lax.fori_loop(0, nd, at, 0)
 
     def work(i):
         zi, ee = source_of(i)
@@ -147,14 +176,41 @@
 
         @pl.when(jnp.logical_not(mine))
         def _():
-            to_pair(zi).start()
-
-            @pl.when(i >= 3)
-            def _():
-                zp, _ = source_of(i - 2)
-                from_pair(zp)
-                sendz[zp] = (keep[zp] + recvy[zp].astype(jnp.float32)).astype(jnp.bfloat16)
-                to_line(zp).start()
+            chunks(lambda k: to_pair(zi, k).start())
+
+        @pl.when(i == 4)
+        def _():
+            def go(k):
+                zp = lax.rem(near + 2, nz)
+                from_pair(zp, k)
+                sendz[0, chunk(k), :] = both(zp, k).astype(jnp.bfloat16)
+                to_line(0, k, near).start()
+
+            chunks(go)
+
+        @pl.when(i == 6)
+        def _():
+            def go(k):
+                from_pair(far, k)
+                from_line(0, k)
+                sendz[1, chunk(k), :] = (
+                    both(far, k) + recvz[0, chunk(k), :].astype(jnp.float32)
+                ).astype(jnp.bfloat16)
+                to_line(1, k, far).start()
+
+            chunks(go)
+
+        block = g_ref.shape[1]
+        for q in range(po):
+            @pl.loop(0, width // TILE)
+            def _(t):
+                cs = pl.ds(pl.multiple_of(t * TILE, TILE), TILE)
+                g_ref[q, :, cs] += lax.dot_general(
+                    buf[q, span, pl.ds(pl.multiple_of(d * block, block), block)],
+                    buf[q, span, cs],
+                    (((0,), (0,)), ((), ())),
+                    preferred_element_type=jnp.float32,
+                )
 
     load_w.wait()
 
@@ -163,7 +219,7 @@
         def _():
             _, ee = source_of(i)
 
-            @pl.when(i != ne - 2)
+            @pl.when(i != 0)
             def _():
                 arrived(d, ee)
 
@@ -189,46 +245,37 @@
 
     lax.fori_loop(0, ne + 2, step, 0)
 
-    block = g_ref.shape[1]
-    for q in range(po):
-        @pl.loop(0, width // TILE)
-        def _(t):
-            cs = pl.ds(pl.multiple_of(t * TILE, TILE), TILE)
-            g_ref[q, :, cs] = lax.dot_general(
-                buf[q, :, pl.ds(pl.multiple_of(d * block, block), block)],
-                buf[q, :, cs],
-                (((0,), (0,)), ((), ())),
-                preferred_element_type=jnp.float32,
-            )
-
-    from_pair(z)
-    for k in range(1, nz):
-        zk = lax.rem(z + k, nz)
-        remote(sendz.at[zk], recvz.at[zk], zsend.at[zk], zrecv.at[zk], d, e).wait_recv()
-
-    @pl.loop(0, nd)
-    def _(k):
-        rs = pl.ds(pl.multiple_of(k * tokens, tokens), tokens)
-        total = keep[z, rs, :] + recvy[z, rs, :].astype(jnp.float32)
-        for j in range(1, nz):
-            total = total + recvz[lax.rem(z + j, nz), rs, :].astype(jnp.float32)
-        fin[k] = total.astype(jnp.bfloat16)
-
-    def to_token(k):
-        dd = lax.rem(d + k, nd)
-        return remote(fin.at[dd], osc.at[d], osend.at[k], orecv.at[d], dd, e)
-
-    for k in range(1, nd):
-        to_token(k).start()
+    def pass_on(k):
+        from_pair(near, k)
+        sendz[2, chunk(k), :] = both(near, k).astype(jnp.bfloat16)
+        to_line(2, k, near).start()
+
+    chunks(pass_on)
+
+    def to_token(dd):
+        return remote(fin.at[dd], osc.at[d], osend.at[dd], orecv.at[d], dd, e)
+
+    def settle(dd):
+        from_pair(z, dd)
+        from_line(1, dd)
+        from_line(2, dd)
+        total = both(z, dd) + recvz[1, chunk(dd), :].astype(jnp.float32)
+        total = total + recvz[2, chunk(dd), :].astype(jnp.float32)
+        fin[dd] = total.astype(jnp.bfloat16)
+
+        @pl.when(dd != d)
+        def _():
+            to_token(dd).start()
+
+    chunks(settle)
     o_ref[:, pl.ds(pl.multiple_of(d * cols, cols), cols)] = fin[d]
     for k in range(1, nd):
         dd = lax.rem(d + k, nd)
-        remote(fin.at[dd], osc.at[dd], osend.at[k], orecv.at[dd], d, e).wait_recv()
+        remote(fin.at[dd], osc.at[dd], osend.at[dd], orecv.at[dd], d, e).wait_recv()
         o_ref[:, pl.ds(pl.multiple_of(dd * cols, cols), cols)] = osc[dd]
 
-    for i in range(ne):
-        if i != ne - 2:
-            first(i).wait_send()
+    for i in range(1, ne):
+        first(i).wait_send()
 
     def drain(i, carry):
         _, ee = source_of(i)
@@ -239,12 +286,16 @@
         return carry
 
     lax.fori_loop(0, ne, drain, 0)
-    for k in range(nz):
-        to_pair(k).wait_send()
-    for k in range(1, nz):
-        to_line(lax.rem(z + k, nz)).wait_send()
+    def sent(k):
+        for zi in range(nz):
+            to_pair(zi, k).wait_send()
+        to_line(0, k, near).wait_send()
+        to_line(1, k, far).wait_send()
+        to_line(2, k, near).wait_send()
+
+    chunks(sent)
     for k in range(1, nd):
-        to_token(k).wait_send()
+        to_token(lax.rem(d + k, nd)).wait_send()
 
 
 def positions(routes, experts):
@@ -299,15 +350,15 @@
             pltpu.VMEM((nz, group, cols), bf),
             pltpu.VMEM((nz, group, cols), bf),
             pltpu.VMEM((nz, group, cols), f32),
-            pltpu.VMEM((nz, group, cols), bf),
-            pltpu.VMEM((nz, group, cols), bf),
+            pltpu.VMEM((3, group, cols), bf),
+            pltpu.VMEM((3, group, cols), bf),
             pltpu.VMEM((nd, tokens, cols), bf),
             pltpu.VMEM((nd, tokens, cols), bf),
             pltpu.VMEM((po, nd * cap, group), bf),
             pltpu.VMEM((po, nd * cap, group), bf),
             dma, dma,
             dma((ne,)), dma((ne, max(nx - 1, 1))), dma((ne, nx)), dma((ne * nd,)),
-            dma((nz,)), dma((nz,)), dma((nz,)), dma((nz,)), dma((nd,)), dma((nd,)),
+            dma((nz, nd)), dma((nz, nd)), dma((3, nd)), dma((3, nd)), dma((nd,)), dma((nd,)),
         ],
         compiler_params=pltpu.CompilerParams(
             collective_id=0, has_side_effects=True, vmem_limit_bytes=VMEM_LIMIT
@@ -380,7 +431,7 @@
     po, _, cols = down_weight.shape
     cap = 3 * tokens * top_count // (2 * ne * po)
     group = nd * tokens
-    if cap % 16 or tokens % 16 or nd % 2 or ne % 2 or ne < 4 or tokens > 256:
+    if cap % 16 or tokens % 16 or nd % 2 or ne != 8 or tokens > 256:
         return False
     if width % TILE or cols % TILE or (width // nd) % 128:
         return False

time: 152 us -> 159 us (1.046)
  Pallas kernels: 136 us -> 142 us
    pallas_call x1, Pallas kernels: 136 us -> 142 us  [fused(): pl.pallas_call(functools.partial(fused_kernel, nd, ne, tokens, cap, width...]
where the time goes in v2:
time: 159 us; the launch traced here: 158 us
  Pallas kernels  142 us (89%)
  other arithmetic  7.98 us (5%)
  matrix products  4.5 us (3%)
  local copies, waits for them, and re-layouts  3.19 us (2%)
    pallas_call x1, Pallas kernels, fused(): pl.pallas_call(functools.partial(fused_kernel, nd, ne, tokens, cap, width...  142 us
    div x1, other arithmetic, fused(): return (out, gram / count[:, :1, :1])  5.19 us
    dot_general x1, matrix products, fused(): jnp.dot(pick, packed, preferred_element_type=jnp.float32)  4.5 us

profile of v2, /device:TPU:1, one launch (start us, length us, event | category | flops | bytes accessed | tf_op | source)
XLA Modules:
  0.0 158.4 jit_solution(14494002426368911036)
XLA Ops:
  0.6 0.7 convert_reduce_fusion
  1.3 0.1 pad.10.clone
  1.4 0.7 convert_divide_fusion
  2.1 0.1 copy.9
  2.2 0.1 reshape.111
  2.3 0.1 maximum_maximum_fusion
  2.4 0.8 copy.6
  3.2 0.1 reshape.108
  3.2 0.1 eq.40
  3.4 1.2 reduce-window.6
  4.5 0.2 slice_reduce_fusion
  4.8 0.1 fusion.10
  4.9 0.2 copy.11
  5.1 4.5 %convolution_convert_fusion = bf16[768,1664]{1,0:T(8,128)(2,1)} fusion(bf16[512,4]{1,0:T(8,128)(2,1)S(1)} %copy.11, bf16[512,1536]{1,0:T(8,128)(2,1)} %bitcast.23, s32[512]{0:T(512)S(1)} %multiply_add_fusion), kind=kOutput, calls=%fused_computation.2 | convolution fusion | flops 1315405824 | bytes 4134912 | tf_op jit(solution)/shard_map/dot_general | solution.py:330
  9.6 142.0 %shard_map.59 = (bf16[64,4096]{1,0:T(8,128)(2,1)}, f32[2,384,1536]{2,1,0:T(8,128)}, f32[2,8,128]{2,1,0:T(8,128)}) custom-call(bf16[16,48,1664]{2,1,0:T(8,128)(2,1)} %bitcast.22, bf16[2,1536,1024]{2,1,0:T(8,128)(2,1)} %w_hbm.1), custom_call_target="tpu_custom_call" | custom-call | tf_op jit(solution)/shard_map/pallas_call | solution.py:338
  151.6 0.8 slice_reduce_fusion.1
  152.4 0.0 copy-start
  152.4 5.2 %broadcast_divide_fusion = f32[2,384,1536]{2,1,0:T(8,128)} fusion(f32[2,384,1536]{2,1,0:T(8,128)} %get-tuple-element.6, f32[2]{0:T(128)S(1)} %slice_reduce_fusion.1), kind=kLoop, calls=%fused_computation.3 | loop fusion | flops 1179648 | bytes 9437192 | tf_op jit(solution)/shard_map/div | solution.py:367
  157.6 0.0 copy-done
  157.6 0.8 copy.15
  (6 shorter events, 0.1 us)
Async XLA Ops:
  152.4 5.2 %copy-start = (bf16[64,4096]{1,0:T(8,128)(2,1)S(1)}, bf16[64,4096]{1,0:T(8,128)(2,1)}, u32[]{:S(2)}) copy-start(bf16[64,4096]{1,0:T(8,128)(2,1)} %get-tuple-element.12) | copy-start | bytes 1572868
